TPU v7x, 256 devices: a whole 4x4x8 slice. The times are simulated.
256 devices in a mesh: section: 2 (over core), grp: 4 (over x), dev: 32 (over y, z).
Axes of the slice: x: 4, y: 4, z: 8, core: 2. Of those that a mesh axis runs over, the one named last changes fastest.
Arguments:
- frames: bfloat16 [4, 512, 512, 256], P('grp', 'dev', 'section'), may hold values from -6 to 6
- templates: bfloat16 [8192, 256], P('dev'), may hold values from -0.375 to 0.375
- pair_block: int32 [2, 4, 256], P('section', 'grp', 'dev'), may hold values from 0 to 63
- pair_tile: int32 [2, 4, 256], P('section', 'grp', 'dev'), may hold values from 0 to 3
- pair_count: int32 [2, 4, 32], P('section', 'grp', 'dev'), may hold values from 1 to 8, 128 in all within a row
- owner_order: int32 [8192], replicated, may hold values from 0 to 8191, each once
Outputs:
- quantities: float32 [4, 8192], P('grp', 'dev')
Inputs may be any that keep to these rules, and one draw needn't show every extreme that they name: `pair_count`: each device's count of live slots; the counts of one section half and run sum to half of all slots there, and one of them is 8. `owner_order`: A permutation of the precursors.
All inputs are finite; a program needn't handle non-finite values.
Results may differ from a plain program's by a relative error of at most 0.00037.
Values may be sent and summed in bfloat16 or wider, within the bound.
A program may use at most 64 MiB of HBM per device.

v0:
```python
import math
import jax
import jax.numpy as jnp
from jax import lax
from jax.sharding import PartitionSpec as P

MOB = 512
SCALES = 6
RAD = 4
TM = 64
PB = 128
PREC = 8192
retention_spread = 2.0


def extended(cells, sides, width):
    for axis, dim in sides:
        count = lax.axis_size(axis)
        ends = count - 1
        head = lax.slice_in_dim(cells, 0, width, axis=dim)
        tail = lax.slice_in_dim(cells, cells.shape[dim] - width, cells.shape[dim], axis=dim)
        cells = jnp.concatenate(
            [
                lax.ppermute(tail, axis, [(i, (i + 1) % count) for i in range(ends)]),
                cells,
                lax.ppermute(head, axis, [((i + 1) % count, i) for i in range(ends)]),
            ],
            axis=dim,
        )
    return cells


def retention_weights():
    bell_values = [
        math.exp(-0.5 * (offset / retention_spread) ** 2) for offset in range(-RAD, RAD + 1)
    ]
    bell_total = sum(bell_values)
    return [weight_value / bell_total for weight_value in bell_values]


def mobility_kernels(row_start, row_count):
    row_place = (row_start + jnp.arange(row_count, dtype=jnp.int32)).astype(jnp.float32)
    col_place = jnp.arange(MOB, dtype=jnp.int32).astype(jnp.float32)
    distance = row_place[:, None] - col_place[None, :]
    tables = []
    for level in range(SCALES):
        spread_scans = 2.0**level
        scaled = distance / spread_scans
        tables.append(
            (1.0 - scaled * scaled)
            * jnp.exp(-0.5 * scaled * scaled)
            / math.sqrt(0.75 * math.sqrt(math.pi) * spread_scans)
        )
    return jnp.stack(tables).astype(jnp.bfloat16)


def on_device(frames, templates, pair_block, pair_tile, pair_count, owner_order):
    section_index = lax.axis_index("section")
    weights = retention_weights()
    count_frames = frames.shape[1]
    mob_local = frames.shape[2]
    channels = frames.shape[3]
    framed = extended(frames, (("dev", 1),), RAD)
    padded = framed.astype(jnp.float32)
    smoothed = weights[0] * padded[:, 0:count_frames]
    for offset in range(1, 2 * RAD + 1):
        smoothed = smoothed + weights[offset] * padded[:, offset : offset + count_frames]
    smoothed = smoothed.astype(jnp.bfloat16)
    gathered = lax.all_gather(smoothed, "section", axis=2, tiled=True)
    kernels = mobility_kernels(section_index * mob_local, mob_local)
    wavelet_stack = jnp.einsum(
        "smn,fnc->smfc", kernels, gathered[0], preferred_element_type=jnp.float32
    ).astype(jnp.bfloat16)
    template_panel = lax.all_gather(templates, "dev", axis=0, tiled=True)
    blocks = template_panel.shape[0] // PB
    live_pairs = pair_count[0, 0, 0]
    block_ids = pair_block[0, 0]
    tile_ids = pair_tile[0, 0]

    def visit_pair(slot_index, totals):
        block_id = block_ids[slot_index]
        tile_id = tile_ids[slot_index]
        tile_cells = lax.dynamic_slice_in_dim(wavelet_stack, tile_id * TM, TM, 1).reshape(
            -1, channels
        )
        block_rows = lax.dynamic_slice_in_dim(template_panel, block_id * PB, PB, 0)
        scores = jnp.dot(tile_cells, block_rows.T, preferred_element_type=jnp.float32)
        response = jnp.mean(jnp.maximum(scores, 0.0), axis=0)
        block_hit = (jnp.arange(blocks, dtype=jnp.int32) == block_id).astype(jnp.float32)
        return totals + block_hit[:, None] * response[None, :]

    totals = lax.fori_loop(0, live_pairs, visit_pair, jnp.zeros((blocks, PB), jnp.float32))
    placed = jnp.zeros((PREC,), jnp.float32).at[owner_order].set(totals.reshape(-1))[None]
    summed = lax.psum(placed, "section")
    owned = lax.psum_scatter(summed, "dev", scatter_dimension=1, tiled=True)
    run_count = lax.axis_size("grp")
    run_mask = (jnp.arange(run_count, dtype=jnp.int32) == lax.axis_index("grp")).astype(jnp.float32)
    run_totals = lax.psum(run_mask * jnp.sum(owned), ("grp", "dev"))
    own_total = jnp.sum(run_totals * run_mask)
    factor = jnp.mean(run_totals) / own_total
    return owned * factor


def solution(mesh):
    placed = (
        P("grp", "dev", "section", None),
        P("dev", None),
        P("section", "grp", "dev"),
        P("section", "grp", "dev"),
        P("section", "grp", "dev"),
        P(),
    )
    return jax.shard_map(
        on_device, mesh=mesh, in_specs=placed, out_specs=P("grp", "dev"), check_vma=False
    )
```

profile of v0, /device:TPU:0, one launch (start us, length us, event | category | flops | bytes accessed | tf_op | source)
XLA Modules:
  0.0 833.9 jit_solution(16655650894832102042)
XLA Ops:
  6.5 1.3 fusion.63
  7.8 2.1 collective-permute-start
  9.9 1.3 collective-permute-start.1
  11.2 9.8 %collective-permute-done = bf16[1,4,256,256]{3,2,1,0:T(8,128)(2,1)S(1)} collective-permute-done((bf16[1,4,256,256]{3,2,1,0:T(8,128)(2,1)S(1)}, bf16[1,4,256,256]{3,2,1,0:T(8,128)(2,1)S(1)}, u32[]{:S(2)}, u32[]{:S(2)}) %collective-permute-start) | collective-permute-done | bytes 524320 | tf_op jit(solution)/shard_map/ppermute | solution.py:24
  21.1 4.3 collective-permute-done.1
  25.4 2.1 maximum_convert_fusion
  27.4 5.7 fusion.4
  33.2 0.7 all-gather.5.cloned.1.call-update
  34.3 0.3 fusion.54
  34.8 0.3 fusion.56
  35.0 0.3 fusion.57
  35.3 0.3 fusion.58
  35.6 19.7 %all-gather.3.cloned.1.call-done = bf16[1,16,512,256]{3,2,1,0:T(8,128)(2,1)} async-done(((bf16[1,16,256,256]{3,2,1,0:T(8,128)(2,1)}), bf16[1,16,512,256]{3,2,1,0:T(8,128)(2,1)}) %all-gather.3.cloned.1.call-update) | async-done | bytes 4194320 | tf_op jit(solution)/shard_map/all_gather | solution.py:69
  55.2 11.7 %convolution_convert_fusion = bf16[6,256,16,256]{3,1,2,0:T(8,128)(2,1)} fusion(bf16[1,16,512,256]{3,2,1,0:T(8,128)(2,1)} %all-gather.3.cloned.1.call-done, bf16[6,256,512]{2,1,0:T(8,128)(2,1)S(1)} %fusion.58), kind=kOutput, calls=%fused_computation.9 | convolution fusion | flops 6448742400 | bytes 18350080 | tf_op jit(solution)/shard_map/smn,fnc->smfc/dot_general | solution.py:71
  66.9 73.7 %all-gather.5.cloned.1.call-done = bf16[8192,256]{1,0:T(8,128)(2,1)} async-done(((bf16[256,256]{1,0:T(8,128)(2,1)}), bf16[8192,256]{1,0:T(8,128)(2,1)}) %all-gather.5.cloned.1.call-update) | async-done | bytes 4194320 | tf_op jit(solution)/shard_map/all_gather | solution.py:74
  140.7 10.7 %while.10 = (s32[]{:T(128)}, f32[64,128]{1,0:T(8,128)S(1)}, s32[]{:T(128)}, s32[8]{0:T(128)S(1)}, s32[8]{0:T(128)S(1)}, /*index=5*/bf16[6,256,16,256]{3,1,2,0:T(...) while((s32[]{:T(128)}, f32[64,128]{1,0:T(8,128)S(1)}, ...), condition=%wide.region_2.0_spmd, body=%wide.region_0.0_spmd.sunk | while | flops 404242560 | bytes 15862567 | solution.py:92
  141.4 0.6 dynamic_slice.21
  142.5 2.3 constant_dynamic-slice_fusion.2
  144.8 1.9 copy.14
  146.7 0.6 dynamic_slice.22
  147.9 2.2 fusion.70
  150.1 0.6 compare_convert_fusion.2
  151.4 30.5 %scatter_custom_fusion = f32[8192]{0:T(1024)S(1)} fusion(s32[8192]{0:T(1024)S(1)} %compare_select_fusion, f32[8192]{0:T(1024)S(1)} %bitcast.30, f32[]{:T(128)} %constant.32.clone.1), kind=kCustom, calls=%fused_computation.91 | custom fusion | bytes 32772 | tf_op jit(solution)/shard_map/scatter | solution.py:93
  181.9 2.6 copy.10
  184.6 288.7 %reduce-scatter.4.cloned.1.call-done = f32[256,1]{1,0:T(8,128)} async-done(((f32[8192,1]{1,0:T(8,128)}), f32[256,1]{1,0:T(8,128)}) %reduce-scatter.4.cloned.1.call-update) | async-done | bytes 1040
  473.2 1.0 copy.11
  474.2 2.5 psum.16
  476.7 0.6 reduce_sum.36
  477.3 0.6 compare_select_fusion.2
  477.9 346.8 %psum.15 = f32[4]{0:T(128)S(1)} all-reduce(f32[4]{0:T(128)S(1)} %compare_select_fusion.2), channel_id=1, replica_groups=mesh['section'=2,'grp'=4,'dev'=32] {'grp','dev'}, use_global_device_ids=true, to_apply=%region_7.0 | all-reduce | flops 4 | bytes 32 | tf_op jit(solution)/shard_map/psum | solution.py:98
  824.8 0.7 fusion.62
  826.8 0.6 broadcast_multiply_fusion.1
  (19 shorter events, 0.7 us)
Async XLA Ops:
  6.5 48.7 %all-gather.3.cloned.1.call-start = ((), (), s32[]{:S(2)}) async-start(), calls=%async_computation.1 | async-start | bytes 6291456 | tf_op jit(solution)/shard_map/all_gather | solution.py:69
  7.8 13.3 %collective-permute-start = (bf16[1,4,256,256]{3,2,1,0:T(8,128)(2,1)S(1)}, bf16[1,4,256,256]{3,2,1,0:T(8,128)(2,1)S(1)}, u32[]{:S(2)}, u32[]{:S(2)}) collective-permute-start(bf16[1,4,256,256]{3,2,1,0:T(8,128)(2,1)S(1)} %get-tuple-element.74), channel_id=1, source_target_pairs={{0,1},{1,2},{2,3},{3,4},{4,5},{5,6},{6,7},{7,8},{8,9},{9,10},{10,1... | collective-permute-start | bytes 1572872 | tf_op jit(solution)/shard_map/ppermute | solution.py:24
  9.9 15.4 %collective-permute-start.1 = (bf16[1,4,256,256]{3,2,1,0:T(8,128)(2,1)S(1)}, bf16[1,4,256,256]{3,2,1,0:T(8,128)(2,1)S(1)}, u32[]{:S(2)}, u32[]{:S(2)}) collective-permute-start(bf16[1,4,256,256]{3,2,1,0:T(8,128)(2,1)S(1)} %get-tuple-element.75), channel_id=1, source_target_pairs={{1,0},{2,1},{3,2},{4,3},{5,4},{6,5},{7,6},{8,7},{9,8},{10,9},{11,1... | collective-permute-start | bytes 1572872 | tf_op jit(solution)/shard_map/ppermute | solution.py:26
  27.4 6.6 copy-start
  33.2 107.5 %all-gather.5.cloned.1.call-start = ((), (), s32[]{:S(2)}) async-start(), calls=%async_computation.2 | async-start | bytes 4325376 | tf_op jit(solution)/shard_map/all_gather | solution.py:74
  33.9 439.3 %reduce-scatter.4.cloned.1.call-start = ((), (), s32[]{:S(2)}) async-start(), calls=%async_computation.3 | async-start | bytes 4325376
  35.5 105.1 %copy-start.1 = (s32[1,1,8]{2,1,0:T(1,128)S(1)}, s32[1,1,8]{2,1,0:T(1,128)}, u32[]{:S(2)}) copy-start(s32[1,1,8]{2,1,0:T(1,128)} %param.10) | copy-start | bytes 100
  35.6 105.1 %copy-start.2 = (s32[1,1,8]{2,1,0:T(1,128)S(1)}, s32[1,1,8]{2,1,0:T(1,128)}, u32[]{:S(2)}) copy-start(s32[1,1,8]{2,1,0:T(1,128)} %param.11) | copy-start | bytes 100
Sparse Core Ops, SparseCore 0:
  33.3 21.9 all-gather.2
  57.8 82.8 all-gather.4
  184.7 288.5 reduce-scatter.3
where the time goes:
time: 835 us; the launch traced here: 834 us
  waiting for transfers between devices  397 us (48%)
  blocking collectives  349 us (42%)
  local copies, waits for them, and re-layouts  40.7 us (5%)
  between operations  14.6 us (2%)
  matrix products  13.9 us (2%)
  other arithmetic  12.4 us (1%)
    psum x1, blocking collectives, on_device(): run_totals = lax.psum(run_mask * jnp.sum(owned), ('grp', 'dev'))  347 us
    unnamed x4, waiting for transfers between devices  289 us
    all_gather x1, waiting for transfers between devices, on_device(): template_panel = lax.all_gather(templates, 'dev', axis=0, tiled=True)  73.7 us
    scatter x1, local copies, waits for them, and re-layouts, on_device(): jnp.zeros((PREC,), jnp.float32).at[owner_order].set(totals.reshape(-1))  30.5 us
    all_gather x1, waiting for transfers between devices, on_device(): gathered = lax.all_gather(smoothed, 'section', axis=2, tiled=True)  19.7 us
  transfers between devices with their start and end apart: 5, of which 5 were waited for; matrix products, arithmetic and copies ran while one was open for 2% of the time, Pallas kernels for 0%

commit v1 on v0

--- a/solution.py
+++ b/solution.py
@@ -66,7 +66,8 @@
     for offset in range(1, 2 * RAD + 1):
         smoothed = smoothed + weights[offset] * padded[:, offset : offset + count_frames]
     smoothed = smoothed.astype(jnp.bfloat16)
-    gathered = lax.all_gather(smoothed, "section", axis=2, tiled=True)
+    stack = jnp.stack([smoothed] * lax.axis_size("section"))
+    gathered = jnp.concatenate(lax.all_to_all(stack, "section", 0, 0), axis=2)
     kernels = mobility_kernels(section_index * mob_local, mob_local)
     wavelet_stack = jnp.einsum(
         "smn,fnc->smfc", kernels, gathered[0], preferred_element_type=jnp.float32

time: 835 us -> 789 us (0.945)
  waiting for transfers between devices: 397 us -> 340 us
    all_gather x1, waiting for transfers between devices: 73.7 us -> 41.8 us  [on_device(): template_panel = lax.all_gather(templates, 'dev', axis=0, tiled=True)]
    all_gather x1 -> x0, waiting for transfers between devices: 19.7 us -> none  [on_device(): gathered = lax.all_gather(smoothed, 'section', axis=2, tiled=True)]
    unnamed x4 -> x3, waiting for transfers between devices: 289 us -> 289 us
  transfers between devices with their start and end apart: 5 -> 4, of which waited for: 5 -> 4; matrix products, arithmetic and copies ran while one was open for 2% -> 3% of each run, Pallas kernels for 0% -> 0%
where the time goes in v1:
time: 789 us; the launch traced here: 788 us
  blocking collectives  356 us (45%)
  waiting for transfers between devices  340 us (43%)
  local copies, waits for them, and re-layouts  42.1 us (5%)
  other arithmetic  15.2 us (2%)
  between operations  14.9 us (2%)
  matrix products  13.3 us (2%)
    psum x1, blocking collectives, on_device(): run_totals = lax.psum(run_mask * jnp.sum(owned), ('grp', 'dev'))  347 us
    unnamed x3, waiting for transfers between devices  289 us
    all_gather x1, waiting for transfers between devices, on_device(): template_panel = lax.all_gather(templates, 'dev', axis=0, tiled=True)  41.8 us
    scatter x1, local copies, waits for them, and re-layouts, on_device(): jnp.zeros((PREC,), jnp.float32).at[owner_order].set(totals.reshape(-1))  30.5 us
  transfers between devices with their start and end apart: 4, of which 4 were waited for; matrix products, arithmetic and copies ran while one was open for 3% of the time, Pallas kernels for 0%

profile of v1, /device:TPU:0, one launch (start us, length us, event | category | flops | bytes accessed | tf_op | source)
XLA Modules:
  0.0 787.7 jit_solution(16209346239658800546)
XLA Ops:
  6.5 0.7 all-gather.2.cloned.1.call-update
  7.3 2.3 fusion.63
  9.6 2.1 collective-permute-start
  11.7 1.3 collective-permute-start.1
  13.0 0.9 fusion.59
  13.9 0.9 fusion.54
  14.9 1.0 fusion.55
  15.8 1.0 fusion.56
  16.8 0.8 compare_select_fusion
  17.6 1.0 fusion.57
  18.5 1.0 fusion.58
  19.5 3.6 collective-permute-done
  23.1 4.9 collective-permute-done.1
  28.5 4.7 fusion.12
  33.6 7.1 all_to_all.5
  41.2 11.1 %convolution_convert_fusion = bf16[6,256,16,256]{3,1,2,0:T(8,128)(2,1)} fusion(bf16[16,512,256,1]{2,1,0,3:T(8,128)(2,1)S(1)} %bitcast.34, bf16[6,256,512]{2,1,0:T(8,128)(2,1)} %fusion.58), kind=kOutput, calls=%fused_computation.9 | convolution fusion | flops 6448742400 | bytes 18350080 | tf_op jit(solution)/shard_map/smn,fnc->smfc/dot_general | solution.py:72
  52.3 41.8 %all-gather.2.cloned.1.call-done = bf16[8192,256]{1,0:T(8,128)(2,1)} async-done(((bf16[256,256]{1,0:T(8,128)(2,1)}), bf16[8192,256]{1,0:T(8,128)(2,1)}) %all-gather.2.cloned.1.call-update) | async-done | bytes 4194320 | tf_op jit(solution)/shard_map/all_gather | solution.py:75
  94.0 10.9 %while.10 = (s32[]{:T(128)}, f32[64,128]{1,0:T(8,128)S(1)}, s32[]{:T(128)}, s32[8]{0:T(128)S(1)}, s32[8]{0:T(128)S(1)}, /*index=5*/bf16[6,256,16,256]{3,1,2,0:T(...) while((s32[]{:T(128)}, f32[64,128]{1,0:T(8,128)S(1)}, ...), condition=%wide.region_2.0_spmd, body=%wide.region_0.0_spmd.sunk | while | flops 404242560 | bytes 15862567 | solution.py:93
  94.9 0.6 dynamic_slice.21
  96.0 2.3 constant_dynamic-slice_fusion.2
  98.4 1.9 copy.16
  100.3 0.6 dynamic_slice.22
  101.4 2.2 fusion.71
  105.0 30.5 %scatter_custom_fusion = f32[8192]{0:T(1024)S(1)} fusion(s32[8192]{0:T(1024)S(1)} %compare_select_fusion, f32[8192]{0:T(1024)S(1)} %bitcast.35, f32[]{:T(128)} %constant.32.clone.1), kind=kCustom, calls=%fused_computation.92 | custom fusion | bytes 32772 | tf_op jit(solution)/shard_map/scatter | solution.py:94
  135.4 2.6 copy.12
  138.1 288.6 %reduce-scatter.4.cloned.1.call-done = f32[256,1]{1,0:T(8,128)} async-done(((f32[8192,1]{1,0:T(8,128)}), f32[256,1]{1,0:T(8,128)}) %reduce-scatter.4.cloned.1.call-update) | async-done | bytes 1040
  426.7 1.0 copy.13
  427.7 2.5 psum.16
  430.1 0.6 reduce_sum.36
  430.7 0.6 compare_select_fusion.2
  431.4 346.8 %psum.15 = f32[4]{0:T(128)S(1)} all-reduce(f32[4]{0:T(128)S(1)} %compare_select_fusion.2), channel_id=1, replica_groups=mesh['section'=2,'grp'=4,'dev'=32] {'grp','dev'}, use_global_device_ids=true, to_apply=%region_7.0 | all-reduce | flops 4 | bytes 32 | tf_op jit(solution)/shard_map/psum | solution.py:99
  778.2 0.7 fusion.62
  (19 shorter events, 2.6 us)
Async XLA Ops:
  6.5 21.5 %copy-start = (bf16[1,16,256,256]{3,2,1,0:T(8,128)(2,1)S(1)}, bf16[1,16,256,256]{3,2,1,0:T(8,128)(2,1)}, u32[]{:S(2)}) copy-start(bf16[1,16,256,256]{3,2,1,0:T(8,128)(2,1)} %param.8) | copy-start | bytes 6291460
  6.5 87.5 %all-gather.2.cloned.1.call-start = ((), (), s32[]{:S(2)}) async-start(), calls=%async_computation.2 | async-start | bytes 4325376 | tf_op jit(solution)/shard_map/all_gather | solution.py:75
  7.3 419.4 %reduce-scatter.4.cloned.1.call-start = ((), (), s32[]{:S(2)}) async-start(), calls=%async_computation.3 | async-start | bytes 4325376
  9.6 13.6 %collective-permute-start = (bf16[1,4,256,256]{3,2,1,0:T(8,128)(2,1)}, bf16[1,4,256,256]{3,2,1,0:T(8,128)(2,1)S(1)}, u32[]{:S(2)}, u32[]{:S(2)}) collective-permute-start(bf16[1,4,256,256]{3,2,1,0:T(8,128)(2,1)} %get-tuple-element.74), channel_id=1, source_target_pairs={{0,1},{1,2},{2,3},{3,4},{4,5},{5,6},{6,7},{7,8},{8,9},{9,10},{10,1... | collective-permute-start | bytes 1572872 | tf_op jit(solution)/shard_map/ppermute | solution.py:24
  11.7 16.3 %collective-permute-start.1 = (bf16[1,4,256,256]{3,2,1,0:T(8,128)(2,1)}, bf16[1,4,256,256]{3,2,1,0:T(8,128)(2,1)S(1)}, u32[]{:S(2)}, u32[]{:S(2)}) collective-permute-start(bf16[1,4,256,256]{3,2,1,0:T(8,128)(2,1)} %get-tuple-element.75), channel_id=1, source_target_pairs={{1,0},{2,1},{3,2},{4,3},{5,4},{6,5},{7,6},{8,7},{9,8},{10,9},{11,1... | collective-permute-start | bytes 1572872 | tf_op jit(solution)/shard_map/ppermute | solution.py:26
  41.2 52.9 %copy-start.1 = (s32[1,1,8]{2,1,0:T(1,128)S(1)}, s32[1,1,8]{2,1,0:T(1,128)}, u32[]{:S(2)}) copy-start(s32[1,1,8]{2,1,0:T(1,128)} %param.10) | copy-start | bytes 100
  41.2 52.9 %copy-start.2 = (s32[1,1,8]{2,1,0:T(1,128)S(1)}, s32[1,1,8]{2,1,0:T(1,128)}, u32[]{:S(2)}) copy-start(s32[1,1,8]{2,1,0:T(1,128)} %param.11) | copy-start | bytes 100
Sparse Core Ops, SparseCore 0:
  9.9 84.0 all-gather.1
  138.2 288.4 reduce-scatter.3
